TPU v7x, 512 devices: a whole 4x4x16 slice. The times are simulated.
512 devices in a mesh: fib: 16 (over y, x), blk: 32 (over z, core).
Axes of the slice: x: 4, y: 4, z: 16, core: 2. Of those that a mesh axis runs over, the one named last changes fastest.
Arguments:
- field_data: float32 [33, 64, 512, 256], P(None, 'blk', 'fib'), may hold values from -120 to 120
- start_block: float32 [512, 64], replicated, may hold values from -6 to 6
Outputs:
- core_out: float32 [33, 64, 64, 256], P(None, 'blk', 'fib')
All inputs are finite; a program needn't handle non-finite values.
Results may differ from a plain program's by a relative error of at most 0.00013.
Values sent between devices are 32-bit elements; how exact they have to be, the bound alone decides.
A program may use at most 192 MiB of HBM per device.

v0:
```python
import jax
import jax.numpy as jnp
from jax import lax
from jax.sharding import PartitionSpec as P


def shards(field_data, start_block):
    highest = lax.Precision.HIGHEST
    received = lax.all_to_all(field_data, "fib", split_axis=3, concat_axis=2, tiled=True)
    width_x = received.shape[2]
    unfolded = jnp.transpose(received, (0, 1, 3, 2)).reshape(-1, width_x)
    contract_rows = (((0,), (0,)), ((), ()))
    local_gram = lax.dot_general(unfolded, unfolded, contract_rows, precision=highest)
    gram_total = lax.psum(local_gram, ("fib", "blk"))
    raw_basis = jnp.dot(gram_total, start_block, precision=highest)
    inner_block = jnp.dot(raw_basis.T, raw_basis, precision=highest)
    lower_factor = jnp.linalg.cholesky(inner_block)
    basis_cols = jax.scipy.linalg.solve_triangular(lower_factor, raw_basis.T, lower=True).T
    core_local = jnp.einsum("szxy,xr->szry", received, basis_cols, precision=highest)
    return lax.all_to_all(core_local, "fib", split_axis=2, concat_axis=3, tiled=True)


def solution(mesh):
    in_specs = (P(None, "blk", "fib", None), P())
    out_specs = P(None, "blk", "fib", None)
    return jax.shard_map(shards, mesh=mesh, in_specs=in_specs, out_specs=out_specs, check_vma=False)
```

profile of v0, /device:TPU:1, one launch (start us, length us, event | category | flops | bytes accessed | tf_op | source)
XLA Modules:
  0.0 619.4 jit_solution(7491580162648552195)
XLA Ops:
  6.5 0.0 copy-start
  6.5 0.0 all-reduce.2.cloned.1.call-start
  6.5 8.7 %copy.13 = f32[33,2,32,256]{0,2,1,3:T(8,128)} copy(f32[33,2,32,256]{3,2,1,0:T(8,128)} %param.2) | data formatting | bytes 4325376 | tf_op args[0]
  15.2 10.1 %reshape.13 = f32[16,1,33792]{2,1,0:T(1,128)S(1)} reshape(f32[256,2,32,33]{3,2,1,0:T(8,128)} %bitcast.45) | data formatting | bytes 4325376
  25.3 34.1 %all_to_all.36 = f32[16,1,33792]{2,1,0:T(1,128)} all-to-all(f32[16,1,33792]{2,1,0:T(1,128)S(1)} %reshape.13), channel_id=1, replica_groups=mesh['fib'=16,'blk'=32] {'fib'}, dimensions={0} | all-to-all | bytes 4325376 | tf_op jit(solution)/shard_map/all_to_all | solution.py:9
  59.4 0.5 broadcast.53
  59.9 7.4 %reduce.6 = f32[16,33792]{1,0:T(8,128)S(1)} reduce(f32[16,1,33792]{2,1,0:T(1,128)} %all_to_all.36, f32[]{:T(128)} %broadcast.53), dimensions={1}, to_apply=%all_to_all.26.reduce_sub_computation | reduce | bytes 4325380 | tf_op jit(solution)/shard_map/all_to_all | solution.py:9
  67.3 12.4 %reshape.14 = f32[256,2,32,33]{3,2,1,0:T(8,128)} reshape(f32[16,33792]{1,0:T(8,128)S(1)} %reduce.6) | data formatting | bytes 4325376
  79.8 11.7 %copy.15 = f32[33,2,16,32,16]{3,2,4,1,0:T(8,128)} copy(f32[33,2,16,32,16]{0,3,1,4,2:T(8,128)} %bitcast.46) | data formatting | bytes 4325376 | tf_op jit(solution)/shard_map/all_to_all | solution.py:9
  91.5 6.7 %all_to_all.29 = f32[33,2,512,16]{2,3,1,0:T(8,128)S(1)} reshape(f32[33,2,16,32,16]{3,2,4,1,0:T(8,128)} %copy.15) | data formatting | bytes 4325376 | tf_op jit(solution)/shard_map/all_to_all | solution.py:9
  98.2 5.4 fusion.4
  103.5 0.0 all-reduce.2.cloned.1.call-update
  103.6 470.4 %all-reduce.2.cloned.1.call-done = f32[512,512]{1,0:T(8,128)} async-done(((f32[512,512]{1,0:T(8,128)}), f32[512,512]{1,0:T(8,128)}) %all-reduce.2.cloned.1.call-update) | async-done | bytes 1048592 | tf_op jit(solution)/shard_map/psum | solution.py:14
  574.0 0.0 copy-done
  574.0 2.4 fusion.13
  576.4 0.3 fusion.14
  576.6 0.1 copy.16
  576.7 5.8 cholesky.16
  582.6 0.7 compare_reduce_fusion
  583.3 0.7 fusion.10
  584.0 4.9 custom-call.7
  588.9 0.3 convolution_bitcast_fusion
  589.3 3.0 fusion.7
  592.3 1.0 copy.18
  593.3 1.0 reshape.15
  594.3 14.6 %all_to_all.37 = f32[16,1,4224]{2,1,0:T(1,128)S(1)} all-to-all(f32[16,1,4224]{2,1,0:T(1,128)S(1)} %reshape.15), channel_id=1, replica_groups=mesh['fib'=16,'blk'=32] {'fib'}, dimensions={0} | all-to-all | bytes 540672 | tf_op jit(solution)/shard_map/all_to_all | solution.py:20
  608.9 1.3 reduce.7
  610.2 1.1 reshape.16
  611.4 0.1 copy.20
  611.5 1.0 copy.21
  (2 shorter events, 0.0 us)
Async XLA Ops:
  6.5 567.5 %copy-start = (f32[512,64]{0,1:T(8,128)S(1)}, f32[512,64]{0,1:T(8,128)}, u32[]{:S(2)}) copy-start(f32[512,64]{0,1:T(8,128)} %param.3) | copy-start | bytes 393220
  6.5 567.5 %all-reduce.2.cloned.1.call-start = ((), (), s32[]{:S(2)}) async-start(), calls=%async_computation.2 | async-start | bytes 2097152 | tf_op jit(solution)/shard_map/psum | solution.py:14
Sparse Core Ops, SparseCore 0:
  103.7 470.2 all-reduce.1
where the time goes:
time: 620 us; the launch traced here: 619 us
  waiting for transfers between devices  470 us (76%)
  local copies, waits for them, and re-layouts  54.5 us (9%)
  blocking collectives  48.7 us (8%)
  other arithmetic  20.9 us (3%)
  between operations  13.5 us (2%)
  matrix products  11.3 us (2%)
    psum x1, waiting for transfers between devices, shards(): gram_total = lax.psum(local_gram, ('fib', 'blk'))  470 us
    all_to_all x1, blocking collectives, shards(): lax.all_to_all(field_data, 'fib', split_axis=3, concat_axis=2, tiled=True)  34.1 us
    unnamed x7, local copies, waits for them, and re-layouts  33.4 us
    all_to_all x3, local copies, waits for them, and re-layouts, shards(): lax.all_to_all(field_data, 'fib', split_axis=3, concat_axis=2, tiled=True)  18.9 us
    all_to_all x1, blocking collectives, shards(): lax.all_to_all(core_local, 'fib', split_axis=2, concat_axis=3, tiled=True)  14.6 us
  transfers between devices with their start and end apart: 1, of which 1 were waited for; matrix products, arithmetic and copies ran while one was open for 0% of the time, Pallas kernels for 0%

commit v1 on v0

--- a/solution.py
+++ b/solution.py
@@ -11,7 +11,9 @@
     unfolded = jnp.transpose(received, (0, 1, 3, 2)).reshape(-1, width_x)
     contract_rows = (((0,), (0,)), ((), ()))
     local_gram = lax.dot_general(unfolded, unfolded, contract_rows, precision=highest)
-    gram_total = lax.psum(local_gram, ("fib", "blk"))
+    gram_total = local_gram
+    for mesh_axis in ("blk", "fib"):
+        gram_total = lax.psum(gram_total, mesh_axis)
     raw_basis = jnp.dot(gram_total, start_block, precision=highest)
     inner_block = jnp.dot(raw_basis.T, raw_basis, precision=highest)
     lower_factor = jnp.linalg.cholesky(inner_block)

time: 620 us -> 483 us (0.78)
  waiting for transfers between devices: 470 us -> 334 us
    psum x1 -> x2, waiting for transfers between devices: 470 us -> 334 us  [shards(): gram_total = lax.psum(gram_total, mesh_axis)]
  transfers between devices with their start and end apart: 1 -> 2, of which waited for: 1 -> 2; matrix products, arithmetic and copies ran while one was open for 0% -> 0% of each run, Pallas kernels for 0% -> 0%
where the time goes in v1:
time: 483 us; the launch traced here: 480 us
  waiting for transfers between devices  334 us (69%)
  local copies, waits for them, and re-layouts  54.5 us (11%)
  blocking collectives  45.9 us (10%)
  other arithmetic  20.9 us (4%)
  between operations  13.5 us (3%)
  matrix products  11.3 us (2%)
    psum x2, waiting for transfers between devices, shards(): gram_total = lax.psum(gram_total, mesh_axis)  334 us
    all_to_all x1, blocking collectives, shards(): lax.all_to_all(field_data, 'fib', split_axis=3, concat_axis=2, tiled=True)  34.1 us
    unnamed x7, local copies, waits for them, and re-layouts  33.4 us
    all_to_all x3, local copies, waits for them, and re-layouts, shards(): lax.all_to_all(field_data, 'fib', split_axis=3, concat_axis=2, tiled=True)  18.9 us
    all_to_all x1, blocking collectives, shards(): lax.all_to_all(core_local, 'fib', split_axis=2, concat_axis=3, tiled=True)  11.8 us
  transfers between devices with their start and end apart: 2, of which 2 were waited for; matrix products, arithmetic and copies ran while one was open for 0% of the time, Pallas kernels for 0%

profile of v1, /device:TPU:1, one launch (start us, length us, event | category | flops | bytes accessed | tf_op | source)
XLA Modules:
  0.0 480.0 jit_solution(11304184995907510564)
XLA Ops:
  6.5 0.0 copy-start
  6.5 0.0 all-reduce.3.cloned.1.call-start
  6.5 8.7 %copy.13 = f32[33,2,32,256]{0,2,1,3:T(8,128)} copy(f32[33,2,32,256]{3,2,1,0:T(8,128)} %param.2) | data formatting | bytes 4325376 | tf_op args[0]
  15.2 10.1 %reshape.13 = f32[16,1,33792]{2,1,0:T(1,128)S(1)} reshape(f32[256,2,32,33]{3,2,1,0:T(8,128)} %bitcast.45) | data formatting | bytes 4325376
  25.3 34.1 %all_to_all.36 = f32[16,1,33792]{2,1,0:T(1,128)} all-to-all(f32[16,1,33792]{2,1,0:T(1,128)S(1)} %reshape.13), channel_id=1, replica_groups=mesh['fib'=16,'blk'=32] {'fib'}, dimensions={0} | all-to-all | bytes 4325376 | tf_op jit(solution)/shard_map/all_to_all | solution.py:9
  59.4 0.5 broadcast.53
  59.9 7.4 %reduce.6 = f32[16,33792]{1,0:T(8,128)S(1)} reduce(f32[16,1,33792]{2,1,0:T(1,128)} %all_to_all.36, f32[]{:T(128)} %broadcast.53), dimensions={1}, to_apply=%all_to_all.26.reduce_sub_computation | reduce | bytes 4325380 | tf_op jit(solution)/shard_map/all_to_all | solution.py:9
  67.3 12.4 %reshape.14 = f32[256,2,32,33]{3,2,1,0:T(8,128)} reshape(f32[16,33792]{1,0:T(8,128)S(1)} %reduce.6) | data formatting | bytes 4325376
  79.8 11.7 %copy.15 = f32[33,2,16,32,16]{3,2,4,1,0:T(8,128)} copy(f32[33,2,16,32,16]{0,3,1,4,2:T(8,128)} %bitcast.46) | data formatting | bytes 4325376 | tf_op jit(solution)/shard_map/all_to_all | solution.py:9
  91.5 6.7 %all_to_all.29 = f32[33,2,512,16]{2,3,1,0:T(8,128)S(1)} reshape(f32[33,2,16,32,16]{3,2,4,1,0:T(8,128)} %copy.15) | data formatting | bytes 4325376 | tf_op jit(solution)/shard_map/all_to_all | solution.py:9
  98.2 5.4 %fusion.4 = f32[512,512]{1,0:T(8,128)} fusion(f32[33,2,512,16]{2,3,1,0:T(8,128)S(1)} %all_to_all.29), kind=kOutput, calls=%fused_computation.4 | convolution fusion | flops 3321888768 | bytes 3211264 | tf_op jit(solution)/shard_map/dot_general | solution.py:13
  103.5 0.0 all-reduce.3.cloned.1.call-update
  103.6 0.0 all-reduce.5.cloned.1.call-start
  103.6 214.2 %all-reduce.3.cloned.1.call-done = f32[512,512]{1,0:T(8,128)} async-done(((f32[512,512]{1,0:T(8,128)}), f32[512,512]{1,0:T(8,128)}) %all-reduce.3.cloned.1.call-update) | async-done | bytes 1048592 | tf_op jit(solution)/shard_map/psum | solution.py:16
  317.8 0.0 all-reduce.5.cloned.1.call-update
  317.8 119.6 %all-reduce.5.cloned.1.call-done = f32[512,512]{1,0:T(8,128)} async-done(((f32[512,512]{1,0:T(8,128)}), f32[512,512]{1,0:T(8,128)}) %all-reduce.5.cloned.1.call-update) | async-done | bytes 1048592 | tf_op jit(solution)/shard_map/psum | solution.py:16
  437.4 2.4 fusion.13
  439.8 0.3 fusion.14
  440.1 0.1 copy.16
  440.2 5.8 %cholesky.16 = f32[64,64]{1,0:T(8,128)S(1)} custom-call(f32[64,64]{1,0:T(8,128)S(1)} %fusion.12), custom_call_target="Cholesky" | custom-call | tf_op jit(solution)/shard_map/jit(cholesky)/cholesky | solution.py:19
  446.0 0.7 compare_reduce_fusion
  446.8 0.7 fusion.10
  447.5 4.9 %custom-call.7 = f32[1,64,64]{1,2,0:T(8,128)S(1)} custom-call(f32[1,64,64]{2,1,0:T(8,128)S(1)} %fusion.10), custom_call_target="InvertDiagBlocksLowerTriangular" | custom-call | tf_op jit(solution)/shard_map/jit(_solve_triangular)/triangular_solve | solution.py:20
  452.4 0.3 convolution_bitcast_fusion
  452.7 3.0 fusion.7
  455.7 1.0 copy.18
  456.7 1.0 reshape.15
  457.8 11.8 %all_to_all.37 = f32[16,1,4224]{2,1,0:T(1,128)S(1)} all-to-all(f32[16,1,4224]{2,1,0:T(1,128)S(1)} %reshape.15), channel_id=1, replica_groups=mesh['fib'=16,'blk'=32] {'fib'}, dimensions={0} | all-to-all | bytes 540672 | tf_op jit(solution)/shard_map/all_to_all | solution.py:22
  469.6 1.3 reduce.7
  470.8 1.1 reshape.16
  472.0 0.1 copy.20
  472.1 1.0 copy.21
  (3 shorter events, 0.0 us)
Async XLA Ops:
  6.5 430.9 %copy-start = (f32[512,64]{0,1:T(8,128)S(1)}, f32[512,64]{0,1:T(8,128)}, u32[]{:S(2)}) copy-start(f32[512,64]{0,1:T(8,128)} %param.3) | copy-start | bytes 393220
  6.5 311.3 %all-reduce.3.cloned.1.call-start = ((), (), s32[]{:S(2)}) async-start(), calls=%async_computation.2 | async-start | bytes 2097152 | tf_op jit(solution)/shard_map/psum | solution.py:16
  103.6 333.9 %all-reduce.5.cloned.1.call-start = ((), (), s32[]{:S(2)}) async-start(), calls=%async_computation.3 | async-start | bytes 2097152 | tf_op jit(solution)/shard_map/psum | solution.py:16
Sparse Core Ops, SparseCore 0:
  103.7 214.0 all-reduce.2
  321.4 116.0 all-reduce.4
